TPU v7x, 256 devices: a whole 4x4x8 slice. The times are simulated.
256 devices in a mesh: patch: 32 (over y, z), req: 4 (over x), owner: 2 (over core).
Axes of the slice: x: 4, y: 4, z: 8, core: 2. Of those that a mesh axis runs over, the one named last changes fastest.
Arguments:
- latents: bfloat16 [8, 256, 256, 320], P('req', 'patch', 'owner'), may hold values from -24 to 24
- timestep_embedding: bfloat16 [8, 1280], P('req'), may hold values from -6 to 6
- embedding_weight: bfloat16 [1280, 320], replicated, may hold values from -0.15625 to 0.15625
- group_norm_gain: float32 [2, 320], replicated, may hold values from 0.25 to 1.75
- group_norm_shift: float32 [2, 320], replicated, may hold values from -3 to 3
- kernel_weight: bfloat16 [2, 9, 320, 320], replicated, may hold values from -0.109375 to 0.109375
- plugin_reduce_library: bfloat16 [8, 2, 184320], P(('req', 'owner'), None, 'patch'), may hold values from -0.109375 to 0.109375
- plugin_expand_library: bfloat16 [8, 2, 20480], P(('req', 'owner'), None, 'patch'), may hold values from -0.75 to 0.75
- image_adapter: int32 [8, 1], P('req'), may hold values from 0 to 7
- adapter_bank_row: int32 [8], replicated, may hold values from 0 to 7, each once
Outputs:
- result: bfloat16 [8, 256, 256, 320], P('req', 'patch', 'owner')
Inputs may be any that keep to these rules, and one draw needn't show every extreme that they name: `image_adapter`: each image names one adapter; every adapter is named by some image. A permutation: adapter a is stored in bank row adapter_bank_row[a].
All inputs are finite; a program needn't handle non-finite values.
Results may differ from a plain program's by a relative error of at most 0.0055.
Values may be sent and summed in bfloat16 or wider, within the bound.
A program may use at most 128 MiB of HBM per device.

v0:
```python
import jax
import jax.numpy as jnp
from jax import lax
from jax.sharding import PartitionSpec as P

GROUPS = 32


def padded_2(block, sides, width):
    for axis, dim in sides:
        count = lax.axis_size(axis)
        forward = [(i, i + 1) for i in range(count - 1)]
        backward = [(target, source) for source, target in forward]
        low = lax.ppermute(
            lax.slice_in_dim(block, block.shape[dim] - width, None, axis=dim), axis, forward
        )
        high = lax.ppermute(lax.slice_in_dim(block, 0, width, axis=dim), axis, backward)
        block = jnp.concatenate([low, block, high], axis=dim)
    return block


def group_act(values, gain, shift):
    images, rows, columns, chans = values.shape
    grouped = values.reshape(images, rows, columns, GROUPS, chans // GROUPS)
    count = rows * columns * (chans // GROUPS) * lax.axis_size("patch") * lax.axis_size("owner")
    total = lax.psum(jnp.sum(grouped, axis=(1, 2, 4)), ("patch", "owner"))
    mean = total / count
    centered = grouped - mean[:, None, None, :, None]
    spread = lax.psum(jnp.sum(centered * centered, axis=(1, 2, 4)), ("patch", "owner"))
    var = spread / count
    normed = (centered / jnp.sqrt(var + 1e-05)[:, None, None, :, None]).reshape(values.shape)
    return jax.nn.silu(normed * gain + shift).astype(jnp.bfloat16)


def block_conv(act, kernel, reducing_filter, expanding_linear_map):
    images, rows, columns, chans = act.shape
    outward = kernel.shape[2]
    padded = padded_2(act, (("patch", 1), ("owner", 2)), 1)
    joined = jnp.concatenate(
        [jnp.broadcast_to(kernel[None], (images,) + kernel.shape), reducing_filter], axis=3
    )
    accum = jnp.zeros((images, rows, columns, joined.shape[3]), jnp.float32)
    for tap in range(9):
        row_off, col_off = divmod(tap, 3)
        window = padded[:, row_off : row_off + rows, col_off : col_off + columns, :]
        accum = accum + jnp.einsum(
            "bhwc,bcd->bhwd", window, joined[:, tap], preferred_element_type=jnp.float32
        )
    lowpart = accum[..., outward:].astype(jnp.bfloat16)
    return accum[..., :outward] + jnp.einsum(
        "bhwr,brd->bhwd", lowpart, expanding_linear_map, preferred_element_type=jnp.float32
    )


def local(
    latents,
    timestep_embedding,
    embedding_weight,
    group_norm_gain,
    group_norm_shift,
    kernel_weight,
    plugin_reduce_library,
    plugin_expand_library,
    image_adapter,
    adapter_bank_row,
):
    images, rows, columns, chans = latents.shape
    wanted = image_adapter[:, 0]
    table = jnp.arange(adapter_bank_row.shape[0], dtype=jnp.int32)
    slots = jnp.sum(
        jnp.where(wanted[:, None] == table[None, :], adapter_bank_row[None, :], 0), axis=1
    )
    full_down, full_up = (
        lax.all_gather(plugin_reduce_library, "patch", axis=2, tiled=True),
        lax.all_gather(plugin_expand_library, "patch", axis=2, tiled=True),
    )
    pieces = (
        lax.all_gather(full_down, ("req", "owner"), axis=0, tiled=True),
        lax.all_gather(full_up, ("req", "owner"), axis=0, tiled=True),
    )
    count = pieces[0].shape[0]
    match = (slots[:, None] == jnp.arange(count, dtype=jnp.int32)[None, :]).astype(jnp.bfloat16)
    first = jnp.einsum("ik,kjs->ijs", match, pieces[0], preferred_element_type=jnp.float32)
    second = jnp.einsum("ik,kjs->ijs", match, pieces[1], preferred_element_type=jnp.float32)
    down_sel = first.astype(jnp.bfloat16)
    up_sel = second.astype(jnp.bfloat16)
    rank = up_sel.shape[2] // chans
    down_all = down_sel.reshape(images, 2, 9, chans, rank)
    up_all = up_sel.reshape(images, 2, rank, chans)
    temb = jax.nn.silu(timestep_embedding.astype(jnp.float32)).astype(jnp.bfloat16)
    proj = jnp.dot(temb, embedding_weight, preferred_element_type=jnp.float32)
    source = latents.astype(jnp.float32)
    act1 = group_act(source, group_norm_gain[0], group_norm_shift[0])
    hidden1 = (
        block_conv(act1, kernel_weight[0], down_all[:, 0], up_all[:, 0]) + proj[:, None, None, :]
    ).astype(jnp.bfloat16)
    act2 = group_act(hidden1.astype(jnp.float32), group_norm_gain[1], group_norm_shift[1])
    result = source + block_conv(act2, kernel_weight[1], down_all[:, 1], up_all[:, 1])
    return result.astype(jnp.bfloat16)


def solution(mesh):
    in_specs = (
        P("req", "patch", "owner", None),
        P("req", None),
        P(),
        P(),
        P(),
        P(),
        P(("req", "owner"), None, "patch"),
        P(("req", "owner"), None, "patch"),
        P("req", None),
        P(),
    )
    out_specs = P("req", "patch", "owner", None)
    return jax.shard_map(local, mesh=mesh, in_specs=in_specs, out_specs=out_specs, check_vma=False)
```

profile of v0, /device:TPU:1, one launch (start us, length us, event | category | flops | bytes accessed | tf_op | source)
XLA Modules:
  0.0 778.4 jit_solution(10491722644223189108)
XLA Ops:
  6.6 47.2 %all_gather.12 = bf16[1,2,184320]{2,1,0:T(2,128)(2,1)} all-gather(bf16[1,2,5760]{2,1,0:T(2,128)(2,1)} %param.16), channel_id=1, replica_groups=mesh['patch'=32,'req'=4,'owner'=2] {'patch'}, dimensions={2}, use_global_device_ids=true | all-gather | bytes 760320 | tf_op jit(solution)/shard_map/all_gather | solution.py:74
  55.6 135.6 %psum.28 = f32[2,32]{1,0:T(2,128)S(1)} all-reduce(f32[2,32]{1,0:T(2,128)S(1)} %reduce_sum.59), channel_id=1, replica_groups=mesh['patch'=32,'req'=4,'owner'=2] {'patch','owner'}, use_global_device_ids=true, to_apply=%region_2.3 | all-reduce | flops 64 | bytes 512 | tf_op jit(solution)/shard_map/psum | solution.py:26
  192.2 124.0 %psum.29 = f32[2,32]{1,0:T(2,128)S(1)} all-reduce(f32[2,32]{1,0:T(2,128)S(1)} %reduce_sum.62), channel_id=1, replica_groups=mesh['patch'=32,'req'=4,'owner'=2] {'patch','owner'}, use_global_device_ids=true, to_apply=%region_5.6 | all-reduce | flops 64 | bytes 512 | tf_op jit(solution)/shard_map/psum | solution.py:29
  320.5 32.0 %all_gather.14 = bf16[1,2,20480]{2,1,0:T(2,128)(2,1)S(1)} all-gather(bf16[1,2,640]{2,1,0:T(2,128)(2,1)S(1)} %copy-done.16), channel_id=1, replica_groups=mesh['patch'=32,'req'=4,'owner'=2] {'patch'}, dimensions={2}, use_global_device_ids=true | all-gather | bytes 84480 | tf_op jit(solution)/shard_map/all_gather | solution.py:75
  352.5 24.4 %all_gather.15 = bf16[8,2,20480]{2,1,0:T(2,128)(2,1)S(1)} all-gather(bf16[1,2,20480]{2,1,0:T(2,128)(2,1)S(1)} %all_gather.14), channel_id=1, replica_groups=mesh['patch'=32,'req'=4,'owner'=2] {'req','owner'}, dimensions={0}, use_global_device_ids=true | all-gather | bytes 737280 | tf_op jit(solution)/shard_map/all_gather | solution.py:79
  377.0 4.8 slice_bitcast_fusion
  390.1 3.5 collective-permute-start.3
  398.0 5.7 pad_maximum_fusion
  403.7 10.7 %convolution_convert_fusion = bf16[2,2,184320]{2,0,1:T(2,128)(2,1)} fusion(bf16[8,2,184320]{2,1,0:T(2,128)(2,1)} %all-gather.2.cloned.1.call-done, s32[2]{0:T(128)S(1)} %fusion.123), kind=kOutput, calls=%fused_computation | convolution fusion | flops 12533776 | bytes 7372808 | tf_op jit(solution)/shard_map/ik,kjs->ijs/dot_general | solution.py:83
  414.4 4.7 reshape.54
  419.1 3.3 fusion.145
  428.2 2.9 fusion.54
  431.1 2.9 fusion.50
  439.4 2.7 fusion.14
  444.9 9.6 %add_add_fusion.1 = f32[2,8,128,384]{2,3,1,0:T(8,128)} fusion(f32[2,8,128,384]{2,3,1,0:T(8,128)} %fusion.18, f32[2,8,128,384]{2,3,1,0:T(8,128)} %fusion.48, f32[2,8,128,384]{2,3,1,0:T(8,128)} %fusion.50, f32[2,8,128,384]{2,3,1,0:T(8,128)} %fusion.80, f32[2,8,128,384]{2,3,1,0:T(8,128)S(1)} %copy-done.10, f32[2,8,128,384]{2,3,1,0:T(8,128)} %fusion.54, ...), kind=kOutput, calls=%fused_computation.45 | convolution fusion | flops 510590976 | bytes 35520512 | tf_op jit(solution)/shard_map/bhwc,bcd->bhwd/dot_general | solution.py:46
  457.3 122.8 %psum.30 = f32[2,32]{1,0:T(2,128)S(1)} all-reduce(f32[2,32]{1,0:T(2,128)S(1)} %reduce_sum.82), channel_id=1, replica_groups=mesh['patch'=32,'req'=4,'owner'=2] {'patch','owner'}, use_global_device_ids=true, to_apply=%region_9.10 | all-reduce | flops 64 | bytes 512 | tf_op jit(solution)/shard_map/psum | solution.py:26
  581.0 127.5 %psum.31 = f32[2,32]{1,0:T(2,128)S(1)} all-reduce(f32[2,32]{1,0:T(2,128)S(1)} %reduce_sum.85), channel_id=1, replica_groups=mesh['patch'=32,'req'=4,'owner'=2] {'patch','owner'}, use_global_device_ids=true, to_apply=%region_12.13 | all-reduce | flops 64 | bytes 512 | tf_op jit(solution)/shard_map/psum | solution.py:29
  714.9 3.2 fusion.97
  727.7 3.7 collective-permute-start.7
  731.4 4.1 fusion.22
  741.8 5.0 pad_maximum_fusion.1
  752.2 2.9 fusion.40
  755.1 2.9 fusion.36
  760.7 8.9 %add_add_fusion = f32[2,8,128,384]{2,3,1,0:T(8,128)S(1)} fusion(f32[2,8,128,384]{2,3,1,0:T(8,128)} %fusion.26, f32[2,8,128,384]{2,3,1,0:T(8,128)} %fusion.34, f32[2,8,128,384]{2,3,1,0:T(8,128)} %fusion.36, f32[2,8,128,384]{2,3,1,0:T(8,128)S(1)} %copy-done.9, f32[2,8,128,384]{2,3,1,0:T(8,128)} %fusion.38, f32[2,8,128,384]{2,3,1,0:T(8,128)} %fusion.40, ...), kind=kOutput, calls=%fused_computation.44 | convolution fusion | flops 510590976 | bytes 35520512 | tf_op jit(solution)/shard_map/bhwc,bcd->bhwd/dot_general | solution.py:46
  (124 shorter events, 69.0 us)
Async XLA Ops:
  6.5 375.3 %copy-start = (bf16[1280,320]{0,1:T(8,128)(2,1)S(1)}, bf16[1280,320]{0,1:T(8,128)(2,1)}, u32[]{:S(2)}) copy-start(bf16[1280,320]{0,1:T(8,128)(2,1)} %param.12) | copy-start | bytes 2457604
  6.5 184.9 %copy-start.5 = (bf16[2,8,128,320]{2,3,1,0:T(8,128)(2,1)S(1)}, bf16[2,8,128,320]{2,3,1,0:T(8,128)(2,1)}, u32[]{:S(2)}) copy-start(bf16[2,8,128,320]{2,3,1,0:T(8,128)(2,1)} %param.10) | copy-start | bytes 3932164
  6.5 309.9 %copy-start.15 = (f32[2,320]{1,0:T(2,128)S(1)}, f32[2,320]{1,0:T(2,128)}, u32[]{:S(2)}) copy-start(f32[2,320]{1,0:T(2,128)} %param.13) | copy-start | bytes 7684
  6.5 309.9 %copy-start.14 = (f32[2,320]{1,0:T(2,128)S(1)}, f32[2,320]{1,0:T(2,128)}, u32[]{:S(2)}) copy-start(f32[2,320]{1,0:T(2,128)} %param.14) | copy-start | bytes 7684
  6.5 397.2 %all-gather.2.cloned.1.call-start = ((), (), s32[]{:S(2)}) async-start(), calls=%async_computation | async-start | bytes 6635520 | tf_op jit(solution)/shard_map/all_gather | solution.py:78
  53.8 266.6 %copy-start.16 = (bf16[1,2,640]{2,1,0:T(2,128)(2,1)S(1)}, bf16[1,2,640]{2,1,0:T(2,128)(2,1)}, u32[]{:S(2)}) copy-start(bf16[1,2,640]{2,1,0:T(2,128)(2,1)} %param.17) | copy-start | bytes 7684
  317.9 64.4 %collective-permute-start = (bf16[2,1,128,320]{2,3,1,0:T(8,128)(2,1)S(1)}, bf16[2,1,128,320]{2,3,1,0:T(8,128)(2,1)S(1)}, u32[]{:S(2)}, u32[]{:S(2)}) collective-permute-start(bf16[2,1,128,320]{2,3,1,0:T(8,128)(2,1)S(1)} %get-tuple-element.23), channel_id=1, source_target_pairs={{0,8},{8,16},{16,24},{24,32},{32,40},{40,48},{48,56},{56,64},{64,7... | collective-permute-start | bytes 491528 | tf_op jit(solution)/shard_map/ppermute | solution.py:14
  319.2 63.1 %collective-permute-start.1 = (bf16[2,1,128,320]{2,3,1,0:T(8,128)(2,1)S(1)}, bf16[2,1,128,320]{2,3,1,0:T(8,128)(2,1)S(1)}, u32[]{:S(2)}, u32[]{:S(2)}) collective-permute-start(bf16[2,1,128,320]{2,3,1,0:T(8,128)(2,1)S(1)} %get-tuple-element.24), channel_id=1, source_target_pairs={{8,0},{16,8},{24,16},{32,24},{40,32},{48,40},{56,48},{64,56},{72,6... | collective-permute-start | bytes 491528 | tf_op jit(solution)/shard_map/ppermute | solution.py:17
  377.0 5.1 copy-start.17
  377.0 5.1 copy-start.18
  386.9 7.8 collective-permute-start.2
  390.1 6.3 collective-permute-start.3
  708.7 5.5 copy-start.11
  710.1 9.8 %copy-start.3 = (bf16[2,8,128,320]{2,3,1,0:T(8,128)(2,1)}, bf16[2,8,128,320]{2,3,1,0:T(8,128)(2,1)S(1)}, u32[]{:S(2)}) copy-start(bf16[2,8,128,320]{2,3,1,0:T(8,128)(2,1)S(1)} %multiply_convert_fusion) | copy-start | bytes 3932164
  710.2 7.9 %collective-permute-start.4 = (bf16[2,1,128,320]{2,3,1,0:T(8,128)(2,1)S(1)}, bf16[2,1,128,320]{2,3,1,0:T(8,128)(2,1)S(1)}, u32[]{:S(2)}, u32[]{:S(2)}) collective-permute-start(bf16[2,1,128,320]{2,3,1,0:T(8,128)(2,1)S(1)} %get-tuple-element.21), channel_id=1, source_target_pairs={{0,8},{8,16},{16,24},{24,32},{32,40},{40,48},{48,56},{56,64},{64,7... | collective-permute-start | bytes 491528 | tf_op jit(solution)/shard_map/ppermute | solution.py:14
  712.9 7.0 collective-permute-start.5
  724.4 13.8 %collective-permute-start.6 = (bf16[2,10,1,320]{3,0,2,1:T(2,128)(2,1)S(1)}, bf16[2,10,1,320]{3,0,2,1:T(2,128)(2,1)S(1)}, u32[]{:S(2)}, u32[]{:S(2)}) collective-permute-start(bf16[2,10,1,320]{3,0,2,1:T(2,128)(2,1)S(1)} %copy.104), channel_id=1, source_target_pairs={{0,1},{2,3},{4,5},{6,7},{8,9},{10,11},{12,13},{14,15},{16,17},{18,... | collective-permute-start | bytes 38408 | tf_op jit(solution)/shard_map/ppermute | solution.py:14
  725.7 9.8 %slice-start = ((s8[4423680]{0:T(1024)(128)(4,1)}), s8[229376]{0:T(1024)(128)(4,1)S(1)}, s32[]{:S(2)}) async-start(s8[4423680]{0:T(1024)(128)(4,1)} %bitcast.145), calls=%async_computation.1 | async-start | bytes 458752
  727.7 7.8 %slice-start.1 = ((s8[4423680]{0:T(1024)(128)(4,1)}), s8[4194304]{0:T(1024)(128)(4,1)S(1)}, s32[]{:S(2)}) async-start(s8[4423680]{0:T(1024)(128)(4,1)} %bitcast.145), calls=%async_computation.2 | async-start | bytes 8388608
  727.7 7.8 %copy-start.4 = (bf16[2,8,128,320]{2,3,1,0:T(8,128)(2,1)S(1)}, bf16[2,8,128,320]{2,3,1,0:T(8,128)(2,1)}, u32[]{:S(2)}) copy-start(bf16[2,8,128,320]{2,3,1,0:T(8,128)(2,1)} %copy-done.3) | copy-start | bytes 3932164
  727.7 12.5 %collective-permute-start.7 = (bf16[2,10,1,320]{3,0,2,1:T(2,128)(2,1)S(1)}, bf16[2,10,1,320]{3,0,2,1:T(2,128)(2,1)S(1)}, u32[]{:S(2)}, u32[]{:S(2)}) collective-permute-start(bf16[2,10,1,320]{3,0,2,1:T(2,128)(2,1)S(1)} %copy.109), channel_id=1, source_target_pairs={{1,0},{3,2},{5,4},{7,6},{9,8},{11,10},{13,12},{15,14},{17,16},{19,... | collective-permute-start | bytes 38408 | tf_op jit(solution)/shard_map/ppermute | solution.py:17
  740.1 6.7 slice-start.2
  760.7 8.9 %copy-start.6 = (bf16[2,8,128,320]{2,3,1,0:T(8,128)(2,1)S(1)}, bf16[2,8,128,320]{2,3,1,0:T(8,128)(2,1)}, u32[]{:S(2)}) copy-start(bf16[2,8,128,320]{2,3,1,0:T(8,128)(2,1)} %param.10) | copy-start | bytes 3932164
  760.7 10.6 %copy-start.1 = (bf16[1280,320]{0,1:T(8,128)(2,1)S(1)}, bf16[1280,320]{0,1:T(8,128)(2,1)}, u32[]{:S(2)}) copy-start(bf16[1280,320]{0,1:T(8,128)(2,1)} %param.12) | copy-start | bytes 2457604
  (8 other events, 26.5 us)
Sparse Core Ops, SparseCore 0:
  54.0 51.1 all-gather.1
where the time goes:
time: 784 us; the launch traced here: 778 us
  blocking collectives  614 us (78%)
  matrix products  79 us (10%)
  local copies, waits for them, and re-layouts  37.7 us (5%)
  other arithmetic  17 us (2%)
  starting transfers between devices  15 us (2%)
  between operations  14.1 us (2%)
    psum x2, blocking collectives, group_act(): total = lax.psum(jnp.sum(grouped, axis=(1, 2, 4)), ('patch', 'owner'))  258 us
    psum x2, blocking collectives, group_act(): lax.psum(jnp.sum(centered * centered, axis=(1, 2, 4)), ('patch', 'owner'))  252 us
    dot_general x18, matrix products, block_conv(): jnp.einsum('bhwc,bcd->bhwd', window, joined[:, tap], preferred_element_ty...  62.9 us
    all_gather x1, blocking collectives, local(): lax.all_gather(plugin_reduce_library, 'patch', axis=2, tiled=True)  47.2 us
    all_gather x1, blocking collectives, local(): lax.all_gather(plugin_expand_library, 'patch', axis=2, tiled=True)  32 us
    all_gather x1, blocking collectives, local(): lax.all_gather(full_up, ('req', 'owner'), axis=0, tiled=True)  24.4 us
  transfers between devices with their start and end apart: 9, of which 1 were waited for; matrix products, arithmetic and copies ran while one was open for 5% of the time, Pallas kernels for 0%

commit v1 on v0

--- a/solution.py
+++ b/solution.py
@@ -4,6 +4,32 @@
 from jax.sharding import PartitionSpec as P
 
 GROUPS = 32
+
+
+def fill_run_in(u_in, dim_k):
+    last = list(u_in.shape[1:])
+    last[dim_k] *= u_in.shape[0]
+    return jnp.moveaxis(u_in, 0, dim_k).reshape(last)
+
+
+def check_circles(my_tile, mesh_dim, dim_i=0):
+    size_here = lax.axis_size(mesh_dim)
+    sheets = tuple(((pp, (pp + 1) % size_here) for pp in range(size_here)))
+    so_far_all = tuple(((m, rr) for rr, m in sheets))
+    lower, vec_out = ([], [])
+    for idx in range(size_here - 1):
+        if idx % 2 == 0:
+            small = lax.ppermute(lower[-1] if lower else my_tile, mesh_dim, sheets)
+            lower.append(small)
+        else:
+            b_now = lax.ppermute(vec_out[-1] if vec_out else my_tile, mesh_dim, so_far_all)
+            vec_out.append(b_now)
+    local_now = jnp.stack([*lower[::-1], my_tile, *vec_out], axis=0)
+    block_out = lax.axis_index(mesh_dim)
+    outer = len(lower)
+    x_now = block_out - outer
+    local_now = local_now[(jnp.arange(size_here) - x_now) % size_here]
+    return fill_run_in(local_now, dim_i)
 
 
 def padded_2(block, sides, width):
@@ -76,7 +102,7 @@
     )
     pieces = (
         lax.all_gather(full_down, ("req", "owner"), axis=0, tiled=True),
-        lax.all_gather(full_up, ("req", "owner"), axis=0, tiled=True),
+        check_circles(full_up, ("req", "owner")),
     )
     count = pieces[0].shape[0]
     match = (slots[:, None] == jnp.arange(count, dtype=jnp.int32)[None, :]).astype(jnp.bfloat16)

time: 784 us -> 793 us (1.011)
  blocking collectives: 614 us -> 582 us
  starting transfers between devices: 15 us -> 43 us
    ppermute x0 -> x7, starting transfers between devices: none -> 27.9 us  [the longest x4 27.4 us: check_circles(): small = lax.ppermute(lower[-1] if lower else my_tile, mesh_dim, sheets)]
    all_gather x1 -> x0, blocking collectives: 24.4 us -> none  [local(): lax.all_gather(full_up, ('req', 'owner'), axis=0, tiled=True)]
    psum x2, blocking collectives: 258 us -> 249 us  [group_act(): total = lax.psum(jnp.sum(grouped, axis=(1, 2, 4)), ('patch', 'owner'))]
  transfers between devices with their start and end apart: 9 -> 16, of which waited for: 1 -> 2; matrix products, arithmetic and copies ran while one was open for 5% -> 6% of each run, Pallas kernels for 0% -> 0%
where the time goes in v1:
time: 793 us; the launch traced here: 787 us
  blocking collectives  582 us (73%)
  matrix products  78.8 us (10%)
  local copies, waits for them, and re-layouts  43.3 us (5%)
  starting transfers between devices  43 us (5%)
  other arithmetic  18.8 us (2%)
  between operations  14.2 us (2%)
    psum x2, blocking collectives, group_act(): lax.psum(jnp.sum(centered * centered, axis=(1, 2, 4)), ('patch', 'owner'))  254 us
    psum x2, blocking collectives, group_act(): total = lax.psum(jnp.sum(grouped, axis=(1, 2, 4)), ('patch', 'owner'))  249 us
    dot_general x18, matrix products, block_conv(): jnp.einsum('bhwc,bcd->bhwd', window, joined[:, tap], preferred_element_ty...  62.7 us
    all_gather x1, blocking collectives, local(): lax.all_gather(plugin_reduce_library, 'patch', axis=2, tiled=True)  41.6 us
    all_gather x1, blocking collectives, local(): lax.all_gather(plugin_expand_library, 'patch', axis=2, tiled=True)  37.3 us
    ppermute x4, starting transfers between devices, check_circles(): small = lax.ppermute(lower[-1] if lower else my_tile, mesh_dim, sheets)  27.4 us
  transfers between devices with their start and end apart: 16, of which 2 were waited for; matrix products, arithmetic and copies ran while one was open for 6% of the time, Pallas kernels for 0%

profile of v1, /device:TPU:1, one launch (start us, length us, event | category | flops | bytes accessed | tf_op | source)
XLA Modules:
  0.0 786.6 jit_solution(9320526253211742672)
XLA Ops:
  6.5 37.3 %all_gather.11 = bf16[1,2,20480]{2,1,0:T(2,128)(2,1)S(1)} all-gather(bf16[1,2,640]{2,1,0:T(2,128)(2,1)} %param.17), channel_id=1, replica_groups=mesh['patch'=32,'req'=4,'owner'=2] {'patch'}, dimensions={2}, use_global_device_ids=true | all-gather | bytes 84480 | tf_op jit(solution)/shard_map/all_gather | solution.py:101
  43.8 11.9 %collective-permute-start.4 = (bf16[1,2,20480]{2,1,0:T(2,128)(2,1)S(1)}, bf16[1,2,20480]{2,1,0:T(2,128)(2,1)}, u32[]{:S(2)}, u32[]{:S(2)}) collective-permute-start(bf16[1,2,20480]{2,1,0:T(2,128)(2,1)S(1)} %all_gather.11), channel_id=1, source_target_pairs={{0,1},{1,2},{2,3},{3,4},{4,5},{5,6},{6,7},{7,0},{8,9},{9,10},{10,1... | collective-permute-start | bytes 245768 | tf_op jit(solution)/shard_map/ppermute | solution.py:22
  57.5 125.3 %psum.28 = f32[2,32]{1,0:T(2,128)S(1)} all-reduce(f32[2,32]{1,0:T(2,128)S(1)} %reduce_sum.59), channel_id=1, replica_groups=mesh['patch'=32,'req'=4,'owner'=2] {'patch','owner'}, use_global_device_ids=true, to_apply=%region_2.3 | all-reduce | flops 64 | bytes 512 | tf_op jit(solution)/shard_map/psum | solution.py:52
  184.9 124.8 %psum.29 = f32[2,32]{1,0:T(2,128)S(1)} all-reduce(f32[2,32]{1,0:T(2,128)S(1)} %reduce_sum.62), channel_id=1, replica_groups=mesh['patch'=32,'req'=4,'owner'=2] {'patch','owner'}, use_global_device_ids=true, to_apply=%region_5.6 | all-reduce | flops 64 | bytes 512 | tf_op jit(solution)/shard_map/psum | solution.py:55
  315.3 41.6 %all_gather.9 = bf16[1,2,184320]{2,1,0:T(2,128)(2,1)} all-gather(bf16[1,2,5760]{2,1,0:T(2,128)(2,1)S(1)} %copy-done.13), channel_id=1, replica_groups=mesh['patch'=32,'req'=4,'owner'=2] {'patch'}, dimensions={2}, use_global_device_ids=true | all-gather | bytes 760320 | tf_op jit(solution)/shard_map/all_gather | solution.py:100
  357.0 4.8 slice_bitcast_fusion
  362.4 13.8 %collective-permute-start.5 = (bf16[1,2,20480]{2,1,0:T(2,128)(2,1)}, bf16[1,2,20480]{2,1,0:T(2,128)(2,1)S(1)}, u32[]{:S(2)}, u32[]{:S(2)}) collective-permute-start(bf16[1,2,20480]{2,1,0:T(2,128)(2,1)} %collective-permute-done.4), channel_id=1, source_target_pairs={{0,1},{1,2},{2,3},{3,4},{4,5},{5,6},{6,7},{7,0},{8,9},{9,10},{10,1... | collective-permute-start | bytes 245768 | tf_op jit(solution)/shard_map/ppermute | solution.py:22
  384.0 3.7 collective-permute-start.3
  393.3 6.2 pad_maximum_fusion
  404.8 4.2 all-gather.2.cloned.1.call-done
  409.1 10.7 %convolution_convert_fusion = bf16[2,2,184320]{2,0,1:T(2,128)(2,1)} fusion(bf16[8,2,184320]{2,1,0:T(2,128)(2,1)} %all-gather.2.cloned.1.call-done, s32[2]{0:T(128)S(1)} %fusion.123), kind=kOutput, calls=%fused_computation.1 | convolution fusion | flops 12533776 | bytes 7372808 | tf_op jit(solution)/shard_map/ik,kjs->ijs/dot_general | solution.py:109
  419.8 4.7 reshape.118
  424.5 3.3 fusion.147
  433.6 2.9 fusion.54
  436.5 2.9 fusion.50
  450.2 9.6 %add_add_fusion.1 = f32[2,8,128,384]{2,3,1,0:T(8,128)} fusion(f32[2,8,128,384]{2,3,1,0:T(8,128)} %fusion.18, f32[2,8,128,384]{2,3,1,0:T(8,128)} %fusion.48, f32[2,8,128,384]{2,3,1,0:T(8,128)} %fusion.50, f32[2,8,128,384]{2,3,1,0:T(8,128)} %fusion.80, f32[2,8,128,384]{2,3,1,0:T(8,128)S(1)} %copy-done.10, f32[2,8,128,384]{2,3,1,0:T(8,128)} %fusion.54, ...), kind=kOutput, calls=%fused_computation.46 | convolution fusion | flops 510590976 | bytes 35520512 | tf_op jit(solution)/shard_map/bhwc,bcd->bhwd/dot_general | solution.py:72
  462.7 124.2 %psum.30 = f32[2,32]{1,0:T(2,128)S(1)} all-reduce(f32[2,32]{1,0:T(2,128)S(1)} %reduce_sum.82), channel_id=1, replica_groups=mesh['patch'=32,'req'=4,'owner'=2] {'patch','owner'}, use_global_device_ids=true, to_apply=%region_9.10 | all-reduce | flops 64 | bytes 512 | tf_op jit(solution)/shard_map/psum | solution.py:52
  587.8 129.0 %psum.31 = f32[2,32]{1,0:T(2,128)S(1)} all-reduce(f32[2,32]{1,0:T(2,128)S(1)} %reduce_sum.85), channel_id=1, replica_groups=mesh['patch'=32,'req'=4,'owner'=2] {'patch','owner'}, use_global_device_ids=true, to_apply=%region_12.13 | all-reduce | flops 64 | bytes 512 | tf_op jit(solution)/shard_map/psum | solution.py:55
  723.2 3.2 fusion.97
  736.0 3.7 collective-permute-start.14
  739.7 4.1 fusion.22
  750.1 5.0 pad_maximum_fusion.1
  760.5 2.9 fusion.40
  768.9 8.9 %add_add_fusion = f32[2,8,128,384]{2,3,1,0:T(8,128)S(1)} fusion(f32[2,8,128,384]{2,3,1,0:T(8,128)} %fusion.26, f32[2,8,128,384]{2,3,1,0:T(8,128)} %fusion.34, f32[2,8,128,384]{2,3,1,0:T(8,128)} %fusion.36, f32[2,8,128,384]{2,3,1,0:T(8,128)S(1)} %copy-done.9, f32[2,8,128,384]{2,3,1,0:T(8,128)} %fusion.38, f32[2,8,128,384]{2,3,1,0:T(8,128)} %fusion.40, ...), kind=kOutput, calls=%fused_computation.45 | convolution fusion | flops 510590976 | bytes 35520512 | tf_op jit(solution)/shard_map/bhwc,bcd->bhwd/dot_general | solution.py:72
  (148 shorter events, 83.8 us)
Async XLA Ops:
  6.5 355.3 %copy-start = (bf16[1280,320]{0,1:T(8,128)(2,1)S(1)}, bf16[1280,320]{0,1:T(8,128)(2,1)}, u32[]{:S(2)}) copy-start(bf16[1280,320]{0,1:T(8,128)(2,1)} %param.12) | copy-start | bytes 2457604
  6.5 304.8 %copy-start.5 = (bf16[2,8,128,320]{2,3,1,0:T(8,128)(2,1)S(1)}, bf16[2,8,128,320]{2,3,1,0:T(8,128)(2,1)}, u32[]{:S(2)}) copy-start(bf16[2,8,128,320]{2,3,1,0:T(8,128)(2,1)} %param.10) | copy-start | bytes 3932164
  6.5 308.8 %copy-start.13 = (bf16[1,2,5760]{2,1,0:T(2,128)(2,1)S(1)}, bf16[1,2,5760]{2,1,0:T(2,128)(2,1)}, u32[]{:S(2)}) copy-start(bf16[1,2,5760]{2,1,0:T(2,128)(2,1)} %param.16) | copy-start | bytes 69124
  6.5 402.5 %all-gather.2.cloned.1.call-start = ((), (), s32[]{:S(2)}) async-start(), calls=%async_computation | async-start | bytes 6635520 | tf_op jit(solution)/shard_map/all_gather | solution.py:104
  43.8 318.5 %collective-permute-start.4 = (bf16[1,2,20480]{2,1,0:T(2,128)(2,1)S(1)}, bf16[1,2,20480]{2,1,0:T(2,128)(2,1)}, u32[]{:S(2)}, u32[]{:S(2)}) collective-permute-start(bf16[1,2,20480]{2,1,0:T(2,128)(2,1)S(1)} %all_gather.11), channel_id=1, source_target_pairs={{0,1},{1,2},{2,3},{3,4},{4,5},{5,6},{6,7},{7,0},{8,9},{9,10},{10,1... | collective-permute-start | bytes 245768 | tf_op jit(solution)/shard_map/ppermute | solution.py:22
  55.7 320.4 %collective-permute-start.8 = (bf16[1,2,20480]{2,1,0:T(2,128)(2,1)S(1)}, bf16[1,2,20480]{2,1,0:T(2,128)(2,1)}, u32[]{:S(2)}, u32[]{:S(2)}) collective-permute-start(bf16[1,2,20480]{2,1,0:T(2,128)(2,1)S(1)} %all_gather.11), channel_id=1, source_target_pairs={{1,0},{2,1},{3,2},{4,3},{5,4},{6,5},{7,6},{0,7},{9,8},{10,9},{11,1... | collective-permute-start | bytes 245768 | tf_op jit(solution)/shard_map/ppermute | solution.py:25
  312.7 63.4 %collective-permute-start = (bf16[2,1,128,320]{2,3,1,0:T(8,128)(2,1)S(1)}, bf16[2,1,128,320]{2,3,1,0:T(8,128)(2,1)S(1)}, u32[]{:S(2)}, u32[]{:S(2)}) collective-permute-start(bf16[2,1,128,320]{2,3,1,0:T(8,128)(2,1)S(1)} %get-tuple-element.23), channel_id=1, source_target_pairs={{0,8},{8,16},{16,24},{24,32},{32,40},{40,48},{48,56},{56,64},{64,7... | collective-permute-start | bytes 491528 | tf_op jit(solution)/shard_map/ppermute | solution.py:40
  314.0 62.1 %collective-permute-start.1 = (bf16[2,1,128,320]{2,3,1,0:T(8,128)(2,1)S(1)}, bf16[2,1,128,320]{2,3,1,0:T(8,128)(2,1)S(1)}, u32[]{:S(2)}, u32[]{:S(2)}) collective-permute-start(bf16[2,1,128,320]{2,3,1,0:T(8,128)(2,1)S(1)} %get-tuple-element.24), channel_id=1, source_target_pairs={{8,0},{16,8},{24,16},{32,24},{40,32},{48,40},{56,48},{64,56},{72,6... | collective-permute-start | bytes 491528 | tf_op jit(solution)/shard_map/ppermute | solution.py:43
  362.4 25.3 %collective-permute-start.5 = (bf16[1,2,20480]{2,1,0:T(2,128)(2,1)}, bf16[1,2,20480]{2,1,0:T(2,128)(2,1)S(1)}, u32[]{:S(2)}, u32[]{:S(2)}) collective-permute-start(bf16[1,2,20480]{2,1,0:T(2,128)(2,1)} %collective-permute-done.4), channel_id=1, source_target_pairs={{0,1},{1,2},{2,3},{3,4},{4,5},{5,6},{6,7},{7,0},{8,9},{9,10},{10,1... | collective-permute-start | bytes 245768 | tf_op jit(solution)/shard_map/ppermute | solution.py:22
  376.1 11.6 %collective-permute-start.9 = (bf16[1,2,20480]{2,1,0:T(2,128)(2,1)}, bf16[1,2,20480]{2,1,0:T(2,128)(2,1)S(1)}, u32[]{:S(2)}, u32[]{:S(2)}) collective-permute-start(bf16[1,2,20480]{2,1,0:T(2,128)(2,1)} %collective-permute-done.8), channel_id=1, source_target_pairs={{1,0},{2,1},{3,2},{4,3},{5,4},{6,5},{7,6},{0,7},{9,8},{10,9},{11,1... | collective-permute-start | bytes 245768 | tf_op jit(solution)/shard_map/ppermute | solution.py:25
  380.8 7.4 collective-permute-start.2
  384.0 5.9 collective-permute-start.3
  387.7 3.9 collective-permute-start.6
  387.7 14.1 %collective-permute-start.10 = (bf16[1,2,20480]{2,1,0:T(2,128)(2,1)S(1)}, bf16[1,2,20480]{2,1,0:T(2,128)(2,1)S(1)}, u32[]{:S(2)}, u32[]{:S(2)}) collective-permute-start(bf16[1,2,20480]{2,1,0:T(2,128)(2,1)S(1)} %collective-permute-done.9), channel_id=1, source_target_pairs={{1,0},{2,1},{3,2},{4,3},{5,4},{6,5},{7,6},{0,7},{9,8},{10,9},{11,1... | collective-permute-start | bytes 245768 | tf_op jit(solution)/shard_map/ppermute | solution.py:25
  391.5 8.0 %collective-permute-start.7 = (bf16[1,2,20480]{2,1,0:T(2,128)(2,1)S(1)}, bf16[1,2,20480]{2,1,0:T(2,128)(2,1)S(1)}, u32[]{:S(2)}, u32[]{:S(2)}) collective-permute-start(bf16[1,2,20480]{2,1,0:T(2,128)(2,1)S(1)} %collective-permute-done.6), channel_id=1, source_target_pairs={{0,1},{1,2},{2,3},{3,4},{4,5},{5,6},{6,7},{7,0},{8,9},{9,10},{10,1... | collective-permute-start | bytes 245768 | tf_op jit(solution)/shard_map/ppermute | solution.py:22
  459.9 257.2 %copy-start.14 = (f32[320]{0:T(512)S(1)}, f32[320]{0:T(512)}, u32[]{:S(2)}) copy-start(f32[320]{0:T(512)} %get-tuple-element.7) | copy-start | bytes 3844
  459.9 257.2 %copy-start.15 = (f32[320]{0:T(512)S(1)}, f32[320]{0:T(512)}, u32[]{:S(2)}) copy-start(f32[320]{0:T(512)} %get-tuple-element.28) | copy-start | bytes 3844
  718.5 9.8 %copy-start.3 = (bf16[2,8,128,320]{2,3,1,0:T(8,128)(2,1)}, bf16[2,8,128,320]{2,3,1,0:T(8,128)(2,1)S(1)}, u32[]{:S(2)}) copy-start(bf16[2,8,128,320]{2,3,1,0:T(8,128)(2,1)S(1)} %multiply_convert_fusion) | copy-start | bytes 3932164
  718.5 7.9 %collective-permute-start.11 = (bf16[2,1,128,320]{2,3,1,0:T(8,128)(2,1)S(1)}, bf16[2,1,128,320]{2,3,1,0:T(8,128)(2,1)S(1)}, u32[]{:S(2)}, u32[]{:S(2)}) collective-permute-start(bf16[2,1,128,320]{2,3,1,0:T(8,128)(2,1)S(1)} %get-tuple-element.21), channel_id=1, source_target_pairs={{0,8},{8,16},{16,24},{24,32},{32,40},{40,48},{48,56},{56,64},{64,7... | collective-permute-start | bytes 491528 | tf_op jit(solution)/shard_map/ppermute | solution.py:40
  721.3 7.0 collective-permute-start.12
  732.7 13.8 %collective-permute-start.13 = (bf16[2,10,1,320]{3,0,2,1:T(2,128)(2,1)S(1)}, bf16[2,10,1,320]{3,0,2,1:T(2,128)(2,1)S(1)}, u32[]{:S(2)}, u32[]{:S(2)}) collective-permute-start(bf16[2,10,1,320]{3,0,2,1:T(2,128)(2,1)S(1)} %copy.104), channel_id=1, source_target_pairs={{0,1},{2,3},{4,5},{6,7},{8,9},{10,11},{12,13},{14,15},{16,17},{18,... | collective-permute-start | bytes 38408 | tf_op jit(solution)/shard_map/ppermute | solution.py:40
  734.0 9.8 %slice-start = ((s8[4423680]{0:T(1024)(128)(4,1)}), s8[229376]{0:T(1024)(128)(4,1)S(1)}, s32[]{:S(2)}) async-start(s8[4423680]{0:T(1024)(128)(4,1)} %bitcast.164), calls=%async_computation.1 | async-start | bytes 458752
  736.0 12.4 %collective-permute-start.14 = (bf16[2,10,1,320]{3,0,2,1:T(2,128)(2,1)S(1)}, bf16[2,10,1,320]{3,0,2,1:T(2,128)(2,1)S(1)}, u32[]{:S(2)}, u32[]{:S(2)}) collective-permute-start(bf16[2,10,1,320]{3,0,2,1:T(2,128)(2,1)S(1)} %copy.109), channel_id=1, source_target_pairs={{1,0},{3,2},{5,4},{7,6},{9,8},{11,10},{13,12},{15,14},{17,16},{19,... | collective-permute-start | bytes 38408 | tf_op jit(solution)/shard_map/ppermute | solution.py:43
  768.9 10.6 %copy-start.1 = (bf16[1280,320]{0,1:T(8,128)(2,1)S(1)}, bf16[1280,320]{0,1:T(8,128)(2,1)}, u32[]{:S(2)}) copy-start(bf16[1280,320]{0,1:T(8,128)(2,1)} %param.12) | copy-start | bytes 2457604
  (15 other events, 73.5 us)
Sparse Core Ops, SparseCore 0:
  357.1 51.9 all-gather.1
